TPU v7x, 32 devices: a whole 2x2x4 slice. The times are simulated.
32 devices in a mesh: group: 4 (over y, x), tile: 4 (over z), video: 2 (over core).
Axes of the slice: x: 2, y: 2, z: 4, core: 2. Of those that a mesh axis runs over, the one named last changes fastest.
Arguments:
- features: bfloat16 [8, 8, 16, 24, 384], P(('video', 'tile'), 'group'), parts along dimension 0, may hold values from -6 to 6
- group_slot: int32 [4], replicated, may hold values from 0 to 3, each once
- margins: int32 [4, 4], P('tile'), may hold values from 0 to 4, as said below
- norm_gain: float32 [384], replicated, may hold values from 0.1 to 1.9
- kernel: bfloat16 [3, 3, 3, 384, 384], replicated, may hold values from -0.0625 to 0.0625
- conv_bias: float32 [384], replicated, may hold values from -3 to 3
Outputs:
- decoded: bfloat16 [8, 8, 16, 24, 384], P(('video', 'tile'), 'group'), parts along dimension 0
There are 2 independent parts, one for each index of `video`. A program takes and returns all parts, laid end to end along the dimension named above; an argument that names none is the same for every part. Nothing has to cross between parts.
Inputs may be any that keep to these rules, and one draw needn't show every extreme that they name: group_slot is a permutation of 0 to 3. margins[t] is (left, right, up, down) of tile t; a margin is 0 exactly at the image's border and 1 to 4 elsewhere; the margin a tile has toward a neighbour equals the neighbour's margin back; left and right margins depend only on the tile's column, up and down margins are the same for all columns; some margin equals 4.
All inputs are finite; a program needn't handle non-finite values.
Results may differ from a plain program's by a relative error of at most 0.0043.
Values may be sent and summed in bfloat16 or wider, within the bound.
A program may use at most 128 MiB of HBM per device.

v0:
```python
import jax
import jax.numpy as jnp
from jax import lax
from jax.sharding import PartitionSpec as P

M = 4
GRID_R = 2


def passed_along(shard, axis, by):
    peers = lax.axis_size(axis)
    pairs = [(i, i + by) for i in range(peers) if 0 <= i + by < peers]
    return lax.ppermute(shard, axis, pairs)


def activate(values, norm_gain):
    widened = values.astype(jnp.float32)
    inv_norm = lax.rsqrt(jnp.mean(widened * widened, axis=-1, keepdims=True) + 1e-06)
    return jax.nn.silu(widened * inv_norm * norm_gain).astype(jnp.bfloat16)


def convolve(padded, kernel, conv_bias, row_count, col_count):
    frame_count = padded.shape[0] - 2
    channels = padded.shape[-1]
    summed = jnp.zeros((frame_count * row_count * col_count, kernel.shape[-1]), jnp.float32)
    for tap_time in range(3):
        for tap_row in range(3):
            window = padded[tap_time : tap_time + frame_count, tap_row : tap_row + row_count]
            stacked = jnp.concatenate(
                [window[:, :, tap_col : tap_col + col_count] for tap_col in range(3)], axis=-1
            )
            flattened = stacked.reshape(frame_count * row_count * col_count, 3 * channels)
            summed = summed + jnp.dot(
                flattened,
                kernel[tap_time, tap_row].reshape(3 * channels, -1),
                preferred_element_type=jnp.float32,
            )
    return summed.reshape(frame_count, row_count, col_count, -1) + conv_bias


def window_band(core, near, far):
    position = jnp.arange(core + 2 * M, dtype=jnp.int32)
    return (position >= M - near) & (position < M + core + far)


def rim_weight(step, core, near, far):
    position = jnp.arange(core, dtype=jnp.int32)
    if step == 1:
        distance = position + 1
        margin = near
    elif step == -1:
        distance = core - position
        margin = far
    else:
        return jnp.ones((core,), jnp.float32)
    margin_f = margin.astype(jnp.float32)
    return jnp.maximum(margin_f + 1.0 - distance.astype(jnp.float32), 0.0) / (margin_f + 1.0)


def rim_source(step, core):
    if step == 1:
        return (core - M, M, 0)
    if step == -1:
        return (0, M, M + core)
    return (0, core, M)


def panel_source(step, core):
    if step == 1:
        return (M + core, M, 0)
    if step == -1:
        return (0, M, core - M)
    return (M, core, 0)


def blend_add(weighted, weight_sum, panel, step_r, step_c, row_dest, col_dest, reaches):
    core_h = weighted.shape[1]
    core_w = weighted.shape[2]
    row_len = panel.shape[1]
    col_len = panel.shape[2]
    placed = jnp.pad(
        panel.astype(jnp.float32),
        (
            (0, 0),
            (row_dest, core_h - row_dest - row_len),
            (col_dest, core_w - col_dest - col_len),
            (0, 0),
        ),
    )
    weight = (
        rim_weight(step_r, core_h, reaches[2], reaches[3])[:, None]
        * rim_weight(step_c, core_w, reaches[0], reaches[1])[None, :]
    )
    return (weighted + placed * weight[None, :, :, None], weight_sum + weight)


def gather_rims(source_block, grid_cols):
    core_h = source_block.shape[1]
    core_w = source_block.shape[2]
    result = jnp.pad(source_block, ((0, 0), (M, M), (M, M), (0, 0)))
    for step_r in (1, 0, -1):
        for step_c in (1, 0, -1):
            if step_r == 0 and step_c == 0:
                continue
            row_first, row_len, row_dest = rim_source(step_r, core_h)
            col_first, col_len, col_dest = rim_source(step_c, core_w)
            outgoing = source_block[
                :, row_first : row_first + row_len, col_first : col_first + col_len
            ]
            incoming = passed_along(outgoing, "tile", step_r * grid_cols + step_c)
            result = result.at[:, row_dest : row_dest + row_len, col_dest : col_dest + col_len].set(
                incoming
            )
    return result


def local(features, group_slot, margins, norm_gain, kernel, conv_bias):
    own_block = features[0]
    frame_count, core_h, core_w, channels = own_block.shape
    grid_cols = lax.axis_size("tile") // GRID_R
    reaches = margins[0]
    wanted = group_slot[lax.axis_index("group")] - 1
    chosen = jnp.zeros((2, core_h, core_w, channels), jnp.bfloat16)
    pieces = lax.all_gather(own_block[None], "group", axis=0, tiled=True)
    first_dev = jnp.int32(0)
    for offset in range(pieces.shape[0]):
        matches = group_slot[first_dev + offset] == wanted
        chosen = chosen + jnp.where(matches, pieces[offset], jnp.zeros_like(pieces[offset]))
    buffered = gather_rims(jnp.concatenate([chosen, own_block], axis=0), grid_cols)
    activated = activate(buffered, norm_gain)
    padded = jnp.pad(activated, ((0, 0), (1, 1), (1, 1), (0, 0)))
    weighted = jnp.zeros((frame_count, core_h, core_w, channels), jnp.float32)
    weight_sum = jnp.zeros((core_h, core_w), jnp.float32)
    inside = (
        window_band(core_h, reaches[2], reaches[3])[:, None]
        & window_band(core_w, reaches[0], reaches[1])[None, :]
    )
    inside = jnp.pad(inside, 1)
    masked = jnp.where(inside[None, :, :, None], padded, jnp.zeros_like(padded))
    outputs = convolve(masked, kernel, conv_bias, core_h + 2 * M, core_w + 2 * M).astype(
        jnp.bfloat16
    )
    for step_r in (1, 0, -1):
        for step_c in (1, 0, -1):
            row_first, row_len, row_dest = panel_source(step_r, core_h)
            col_first, col_len, col_dest = panel_source(step_c, core_w)
            outgoing = outputs[:, row_first : row_first + row_len, col_first : col_first + col_len]
            if step_r == 0 and step_c == 0:
                incoming = outgoing
            else:
                incoming = passed_along(outgoing, "tile", step_r * grid_cols + step_c)
            weighted, weight_sum = blend_add(
                weighted, weight_sum, incoming, step_r, step_c, row_dest, col_dest, reaches
            )
    return (weighted / weight_sum[None, :, :, None]).astype(jnp.bfloat16)[None]


def solution(mesh):
    return jax.shard_map(
        local,
        mesh=mesh,
        in_specs=(
            P(("video", "tile"), "group", None, None, None),
            P(),
            P("tile", None),
            P(),
            P(),
            P(),
        ),
        out_specs=P(("video", "tile"), "group", None, None, None),
        check_vma=False,
    )
```

profile of v0, /device:TPU:0, one launch (start us, length us, event | category | flops | bytes accessed | tf_op | source)
XLA Modules:
  0.0 182.1 jit_solution(15480783370561871145)
XLA Ops:
  23.2 5.7 %fusion.21 = (bf16[1,1,3,384,384]{4,3,2,1,0:T(8,128)(2,1)}, bf16[1,1,3,384,384]{4,3,2,1,0:T(8,128)(2,1)}, bf16[1,1,3,384,384]{4,3,2,1,0:T(8,128)(2,1)}, bf16[1,1...) fusion(bf16[3,3,3,384,384]{4,3,2,1,0:T(8,128)(2,1)} %param.26), kind=kLoop, calls=%fused_computation.92 | loop fusion | bytes 15925248 | tf_op jit(solution)/shard_map/slice | solution.py:35
  28.9 20.4 %all-gather.2.cloned.1.call-done = bf16[4,2,16,24,384]{4,3,2,1,0:T(8,128)(2,1)} async-done(((bf16[1,2,16,24,384]{4,3,2,1,0:T(8,128)(2,1)}), bf16[4,2,16,24,384]{4,3,2,1,0:T(8,128)(2,1)}) %all-gather.2.cloned.1.call-update) | async-done | bytes 2359312 | tf_op jit(solution)/shard_map/all_gather | solution.py:124
  51.3 4.3 %collective-permute-start.1 = (bf16[4,4,24,384]{3,2,1,0:T(8,128)(2,1)S(1)}, bf16[4,4,24,384]{3,2,1,0:T(8,128)(2,1)S(1)}, u32[]{:S(2)}, u32[]{:S(2)}) collective-permute-start(bf16[4,4,24,384]{3,2,1,0:T(8,128)(2,1)S(1)} %get-tuple-element.150), channel_id=1, source_target_pairs={{0,4},{2,6},{1,5},{3,7},{8,12},{10,14},{9,13},{11,15},{16,20},{18,... | collective-permute-start | bytes 884744 | tf_op jit(solution)/shard_map/ppermute | solution.py:13
  56.4 2.2 %collective-permute-start = (bf16[4,4,4,384]{3,2,1,0:T(4,128)(2,1)S(1)}, bf16[4,4,4,384]{3,2,1,0:T(4,128)(2,1)S(1)}, u32[]{:S(2)}, u32[]{:S(2)}) collective-permute-start(bf16[4,4,4,384]{3,2,1,0:T(4,128)(2,1)S(1)} %get-tuple-element.146), channel_id=1, source_target_pairs={{0,6},{1,7},{8,14},{9,15},{16,22},{17,23},{24,30},{25,31}} | collective-permute-start | bytes 147464 | tf_op jit(solution)/shard_map/ppermute | solution.py:13
  60.1 2.4 %collective-permute-start.2 = (bf16[4,4,4,384]{3,2,1,0:T(4,128)(2,1)}, bf16[4,4,4,384]{3,2,1,0:T(4,128)(2,1)}, u32[]{:S(2)}, u32[]{:S(2)}) collective-permute-start(bf16[4,4,4,384]{3,2,1,0:T(4,128)(2,1)} %get-tuple-element.147), channel_id=1, source_target_pairs={{0,2},{2,4},{4,6},{1,3},{3,5},{5,7},{8,10},{10,12},{12,14},{9,11},... | collective-permute-start | bytes 147464 | tf_op jit(solution)/shard_map/ppermute | solution.py:13
  66.0 7.2 %collective-permute-start.3 = (bf16[4,16,4,384]{3,2,1,0:T(4,128)(2,1)S(1)}, bf16[4,16,4,384]{3,2,1,0:T(4,128)(2,1)}, u32[]{:S(2)}, u32[]{:S(2)}) collective-permute-start(bf16[4,16,4,384]{3,2,1,0:T(4,128)(2,1)S(1)} %get-tuple-element.152), channel_id=1, source_target_pairs={{0,2},{2,4},{4,6},{1,3},{3,5},{5,7},{8,10},{10,12},{12,14},{9,11},... | collective-permute-start | bytes 589832 | tf_op jit(solution)/shard_map/ppermute | solution.py:13
  75.1 2.3 %scatter.29 = bf16[4,24,32,384]{3,2,1,0:T(8,128)(2,1)S(1)} dynamic-update-slice(bf16[4,24,32,384]{3,2,1,0:T(8,128)(2,1)S(1)} %constant_dynamic-update-slice_fusion.4, bf16[4,4,24,384]{3,2,1,0:T(8,128)(2,1)S(1)} %dynamic-slice_select_fusion, s32[]{:T(128)} %constant.276.clone.1, s32[]{:T(128)} %bitcast.10, s32[]{:T(128)} %bitcast.11, s32[]{:T(128)} %constant.276.clone.1) | dynamic-update-slice | bytes 589828 | tf_op jit(solution)/shard_map/scatter | solution.py:111
  79.0 3.4 %dynamic-slice_select_fusion.1 = bf16[4,4,4,384]{3,2,1,0:T(4,128)(2,1)} fusion(bf16[4,4,4,384]{3,2,1,0:T(4,128)(2,1)} %collective-permute-done.2, bf16[4,24,32,384]{3,2,1,0:T(8,128)(2,1)S(1)} %scatter.29, s32[]{:T(128)} %bitcast.12, s32[]{:T(128)} %bitcast.13, pred[]{:T(512)} %and_reduce_fusion), kind=kLoop, calls=%fused_computation.66 | loop fusion | flops 24576 | bytes 147465 | tf_op jit(solution)/shard_map/select.10
  82.3 2.2 %scatter.30 = bf16[4,24,32,384]{3,2,1,0:T(8,128)(2,1)S(1)} dynamic-update-slice(bf16[4,24,32,384]{3,2,1,0:T(8,128)(2,1)S(1)} %scatter.29, bf16[4,4,4,384]{3,2,1,0:T(4,128)(2,1)} %dynamic-slice_select_fusion.1, s32[]{:T(128)} %constant.276.clone.1, s32[]{:T(128)} %bitcast.12, s32[]{:T(128)} %bitcast.13, s32[]{:T(128)} %constant.276.clone.1) | dynamic-update-slice | bytes 98308 | tf_op jit(solution)/shard_map/scatter | solution.py:111
  86.6 8.5 %collective-permute-done.6 = bf16[4,4,24,384]{3,2,1,0:T(8,128)(2,1)S(1)} collective-permute-done((bf16[4,4,24,384]{3,2,1,0:T(8,128)(2,1)S(1)}, bf16[4,4,24,384]{3,2,1,0:T(8,128)(2,1)S(1)}, u32[]{:S(2)}, u32[]{:S(2)}) %collective-permute-start.6) | collective-permute-done | bytes 294944 | tf_op jit(solution)/shard_map/ppermute | solution.py:13
  97.7 2.2 %fusion.7 = bf16[4,24,32,384]{3,2,1,0:T(8,128)(2,1)S(1)} fusion(bf16[4,24,32,384]{3,2,1,0:T(8,128)(2,1)S(1)} %constant_dynamic-update-slice_fusion, f32[384]{0:T(512)} %param.25, f32[4,24,32]{2,1,0:T(8,128)S(1)} %add_rsqrt_fusion), kind=kLoop, calls=%fused_computation.9 | loop fusion | flops 9437184 | bytes 4732416 | tf_op jit(solution)/shard_map/convert_element_type | solution.py:19
  101.5 4.5 %fusion.23 = (bf16[2,24,32,384]{3,2,1,0:T(8,128)(2,1)S(1)}, bf16[2,24,32,384]{3,2,1,0:T(8,128)(2,1)S(1)}, bf16[2,24,32,384]{3,2,1,0:T(8,128)(2,1)}, bf16[2,24,32...) fusion(bf16[4,26,34,384]{3,2,1,0:T(8,128)(2,1)S(1)} %pad_select, ...), kind=kLoop, calls=%fused_computation.94 | loop fusion | bytes 18874368 | tf_op jit(solution)/shard_map/slice | solution.py:30
  105.9 6.3 %fusion.22 = (bf16[2,24,32,384]{3,2,1,0:T(8,128)(2,1)}, bf16[2,24,32,384]{3,2,1,0:T(8,128)(2,1)}, bf16[2,24,32,384]{3,2,1,0:T(8,128)(2,1)}, bf16[2,24,32,384]{3,...) fusion(bf16[4,26,34,384]{3,2,1,0:T(8,128)(2,1)S(1)} %pad_select, ...), kind=kLoop, calls=%fused_computation.93 | loop fusion | bytes 44826624 | tf_op jit(solution)/shard_map/slice | solution.py:30
  112.2 3.4 %pad_maximum_fusion = (bf16[2,24,32,1152]{3,2,1,0:T(8,128)(2,1)S(1)}, bf16[2,24,32,1152]{3,2,1,0:T(8,128)(2,1)S(1)}) fusion(bf16[2,24,32,384]{3,2,1,0:T(8,128)(2,1)} %get-tuple-element.134, bf16[2,24,32,384]{3,2,1,0:T(8,128)(2,1)} %get-tuple-element.135, bf16[2,24,32,384]{3,2,1,0:T(8,128)(2,1)} %get-tuple-element.136, ...), kind=kLoop, calls=%fused_computation.10 | loop fusion | flops 21233664 | bytes 14155776 | tf_op jit(solution)/shard_map/concatenate | solution.py:29
  117.8 3.6 %convolution_add_fusion.7 = f32[1536,384]{1,0:T(8,128)} fusion(f32[1536,384]{1,0:T(8,128)S(1)} %fusion.31, bf16[1536,1152]{1,0:T(8,128)(2,1)S(1)} %bitcast.65, bf16[1152,384]{1,0:T(8,128)(2,1)S(1)} %bitcast.79), kind=kOutput, calls=%fused_computation.27 | convolution fusion | flops 1359544320 | bytes 9142272 | tf_op jit(solution)/shard_map/dot_general | solution.py:33
  124.6 3.9 %convolution_add_fusion.6 = f32[1536,384]{1,0:T(8,128)S(1)} fusion(f32[1536,384]{1,0:T(8,128)} %convolution_add_fusion.7, bf16[1536,1152]{1,0:T(8,128)(2,1)S(1)} %bitcast.66, bf16[1152,384]{1,0:T(8,128)(2,1)S(1)} %bitcast.78), kind=kOutput, calls=%fused_computation.26 | convolution fusion | flops 1359544320 | bytes 9142272 | tf_op jit(solution)/shard_map/dot_general | solution.py:33
  128.5 2.2 %convolution_add_fusion.5 = f32[1536,384]{1,0:T(8,128)S(1)} fusion(f32[1536,384]{1,0:T(8,128)S(1)} %convolution_add_fusion.6, bf16[1536,1152]{1,0:T(8,128)(2,1)S(1)} %bitcast.62, bf16[1152,384]{1,0:T(8,128)(2,1)S(1)} %bitcast.77), kind=kOutput, calls=%fused_computation.25 | convolution fusion | flops 1359544320 | bytes 9142272 | tf_op jit(solution)/shard_map/dot_general | solution.py:33
  131.9 2.2 %convolution_add_fusion.4 = f32[1536,384]{1,0:T(8,128)S(1)} fusion(f32[1536,384]{1,0:T(8,128)S(1)} %convolution_add_fusion.5, bf16[1536,1152]{1,0:T(8,128)(2,1)S(1)} %bitcast.67, bf16[1152,384]{1,0:T(8,128)(2,1)S(1)} %bitcast.76), kind=kOutput, calls=%fused_computation.24 | convolution fusion | flops 1359544320 | bytes 9142272 | tf_op jit(solution)/shard_map/dot_general | solution.py:33
  134.0 2.1 %convolution_add_fusion.3 = f32[1536,384]{1,0:T(8,128)S(1)} fusion(f32[1536,384]{1,0:T(8,128)S(1)} %convolution_add_fusion.4, bf16[1536,1152]{1,0:T(8,128)(2,1)S(1)} %bitcast.63, bf16[1152,384]{1,0:T(8,128)(2,1)S(1)} %bitcast.75), kind=kOutput, calls=%fused_computation.23 | convolution fusion | flops 1359544320 | bytes 9142272 | tf_op jit(solution)/shard_map/dot_general | solution.py:33
  137.4 2.2 %convolution_add_fusion.2 = f32[1536,384]{1,0:T(8,128)S(1)} fusion(f32[1536,384]{1,0:T(8,128)S(1)} %convolution_add_fusion.3, bf16[1536,1152]{1,0:T(8,128)(2,1)S(1)} %bitcast.68, bf16[1152,384]{1,0:T(8,128)(2,1)S(1)} %bitcast.74), kind=kOutput, calls=%fused_computation.22 | convolution fusion | flops 1359544320 | bytes 9142272 | tf_op jit(solution)/shard_map/dot_general | solution.py:33
  139.6 2.1 %convolution_add_fusion.1 = f32[1536,384]{1,0:T(8,128)S(1)} fusion(f32[1536,384]{1,0:T(8,128)S(1)} %convolution_add_fusion.2, bf16[1536,1152]{1,0:T(8,128)(2,1)S(1)} %bitcast.64, bf16[1152,384]{1,0:T(8,128)(2,1)S(1)} %bitcast.73), kind=kOutput, calls=%fused_computation.21 | convolution fusion | flops 1359544320 | bytes 9142272 | tf_op jit(solution)/shard_map/dot_general | solution.py:33
  148.4 4.5 %collective-permute-start.10 = (bf16[2,4,4,384]{3,2,1,0:T(4,128)(2,1)S(1)}, bf16[2,4,4,384]{3,2,1,0:T(4,128)(2,1)S(1)}, u32[]{:S(2)}, u32[]{:S(2)}) collective-permute-start(bf16[2,4,4,384]{3,2,1,0:T(4,128)(2,1)S(1)} %get-tuple-element.140), channel_id=1, source_target_pairs={{0,2},{2,4},{4,6},{1,3},{3,5},{5,7},{8,10},{10,12},{12,14},{9,11},... | collective-permute-start | bytes 73736 | tf_op jit(solution)/shard_map/ppermute | solution.py:13
  156.2 6.9 %collective-permute-start.9 = (bf16[2,4,24,384]{3,2,1,0:T(8,128)(2,1)S(1)}, bf16[2,4,24,384]{3,2,1,0:T(8,128)(2,1)S(1)}, u32[]{:S(2)}, u32[]{:S(2)}) collective-permute-start(bf16[2,4,24,384]{3,2,1,0:T(8,128)(2,1)S(1)} %get-tuple-element.141), channel_id=1, source_target_pairs={{0,4},{2,6},{1,5},{3,7},{8,12},{10,14},{9,13},{11,15},{16,20},{18,... | collective-permute-start | bytes 442376 | tf_op jit(solution)/shard_map/ppermute | solution.py:13
  165.7 7.4 %collective-permute-done.14 = bf16[2,4,24,384]{3,2,1,0:T(8,128)(2,1)S(1)} collective-permute-done((bf16[2,4,24,384]{3,2,1,0:T(8,128)(2,1)S(1)}, bf16[2,4,24,384]{3,2,1,0:T(8,128)(2,1)S(1)}, u32[]{:S(2)}, u32[]{:S(2)}) %collective-permute-start.14) | collective-permute-done | bytes 147488 | tf_op jit(solution)/shard_map/ppermute | solution.py:13
  (102 shorter events, 47.6 us)
Async XLA Ops:
  6.5 42.7 %all-gather.2.cloned.1.call-start = ((), (), s32[]{:S(2)}) async-start(), calls=%async_computation | async-start | bytes 2949120 | tf_op jit(solution)/shard_map/all_gather | solution.py:124
  28.8 22.2 %copy-start = (bf16[1,2,16,24,384]{4,3,2,1,0:T(8,128)(2,1)S(1)}, bf16[1,2,16,24,384]{4,3,2,1,0:T(8,128)(2,1)}, u32[]{:S(2)}) copy-start(bf16[1,2,16,24,384]{4,3,2,1,0:T(8,128)(2,1)} %param.22) | copy-start | bytes 1769476
  51.3 14.7 %collective-permute-start.1 = (bf16[4,4,24,384]{3,2,1,0:T(8,128)(2,1)S(1)}, bf16[4,4,24,384]{3,2,1,0:T(8,128)(2,1)S(1)}, u32[]{:S(2)}, u32[]{:S(2)}) collective-permute-start(bf16[4,4,24,384]{3,2,1,0:T(8,128)(2,1)S(1)} %get-tuple-element.150), channel_id=1, source_target_pairs={{0,4},{2,6},{1,5},{3,7},{8,12},{10,14},{9,13},{11,15},{16,20},{18,... | collective-permute-start | bytes 884744 | tf_op jit(solution)/shard_map/ppermute | solution.py:13
  56.4 8.3 %collective-permute-start = (bf16[4,4,4,384]{3,2,1,0:T(4,128)(2,1)S(1)}, bf16[4,4,4,384]{3,2,1,0:T(4,128)(2,1)S(1)}, u32[]{:S(2)}, u32[]{:S(2)}) collective-permute-start(bf16[4,4,4,384]{3,2,1,0:T(4,128)(2,1)S(1)} %get-tuple-element.146), channel_id=1, source_target_pairs={{0,6},{1,7},{8,14},{9,15},{16,22},{17,23},{24,30},{25,31}} | collective-permute-start | bytes 147464 | tf_op jit(solution)/shard_map/ppermute | solution.py:13
  58.8 37.5 %collective-permute-start.7 = (bf16[4,4,4,384]{3,2,1,0:T(4,128)(2,1)}, bf16[4,4,4,384]{3,2,1,0:T(4,128)(2,1)}, u32[]{:S(2)}, u32[]{:S(2)}) collective-permute-start(bf16[4,4,4,384]{3,2,1,0:T(4,128)(2,1)} %get-tuple-element.145), channel_id=1, source_target_pairs={{6,0},{7,1},{14,8},{15,9},{22,16},{23,17},{30,24},{31,25}} | collective-permute-start | bytes 147464 | tf_op jit(solution)/shard_map/ppermute | solution.py:13
  60.1 17.4 %collective-permute-start.2 = (bf16[4,4,4,384]{3,2,1,0:T(4,128)(2,1)}, bf16[4,4,4,384]{3,2,1,0:T(4,128)(2,1)}, u32[]{:S(2)}, u32[]{:S(2)}) collective-permute-start(bf16[4,4,4,384]{3,2,1,0:T(4,128)(2,1)} %get-tuple-element.147), channel_id=1, source_target_pairs={{0,2},{2,4},{4,6},{1,3},{3,5},{5,7},{8,10},{10,12},{12,14},{9,11},... | collective-permute-start | bytes 147464 | tf_op jit(solution)/shard_map/ppermute | solution.py:13
  62.5 23.3 %collective-permute-start.5 = (bf16[4,4,4,384]{3,2,1,0:T(4,128)(2,1)}, bf16[4,4,4,384]{3,2,1,0:T(4,128)(2,1)}, u32[]{:S(2)}, u32[]{:S(2)}) collective-permute-start(bf16[4,4,4,384]{3,2,1,0:T(4,128)(2,1)} %get-tuple-element.148), channel_id=1, source_target_pairs={{2,0},{4,2},{6,4},{3,1},{5,3},{7,5},{10,8},{12,10},{14,12},{11,9},... | collective-permute-start | bytes 147464 | tf_op jit(solution)/shard_map/ppermute | solution.py:13
  64.6 21.0 %collective-permute-start.4 = (bf16[4,16,4,384]{3,2,1,0:T(4,128)(2,1)S(1)}, bf16[4,16,4,384]{3,2,1,0:T(4,128)(2,1)S(1)}, u32[]{:S(2)}, u32[]{:S(2)}) collective-permute-start(bf16[4,16,4,384]{3,2,1,0:T(4,128)(2,1)S(1)} %get-tuple-element.151), channel_id=1, source_target_pairs={{2,0},{4,2},{6,4},{3,1},{5,3},{7,5},{10,8},{12,10},{14,12},{11,9},... | collective-permute-start | bytes 589832 | tf_op jit(solution)/shard_map/ppermute | solution.py:13
  66.0 18.6 %collective-permute-start.3 = (bf16[4,16,4,384]{3,2,1,0:T(4,128)(2,1)S(1)}, bf16[4,16,4,384]{3,2,1,0:T(4,128)(2,1)}, u32[]{:S(2)}, u32[]{:S(2)}) collective-permute-start(bf16[4,16,4,384]{3,2,1,0:T(4,128)(2,1)S(1)} %get-tuple-element.152), channel_id=1, source_target_pairs={{0,2},{2,4},{4,6},{1,3},{3,5},{5,7},{8,10},{10,12},{12,14},{9,11},... | collective-permute-start | bytes 589832 | tf_op jit(solution)/shard_map/ppermute | solution.py:13
  77.5 17.6 %collective-permute-start.6 = (bf16[4,4,24,384]{3,2,1,0:T(8,128)(2,1)S(1)}, bf16[4,4,24,384]{3,2,1,0:T(8,128)(2,1)S(1)}, u32[]{:S(2)}, u32[]{:S(2)}) collective-permute-start(bf16[4,4,24,384]{3,2,1,0:T(8,128)(2,1)S(1)} %get-tuple-element.149), channel_id=1, source_target_pairs={{4,0},{6,2},{5,1},{7,3},{12,8},{14,10},{13,9},{15,11},{20,16},{22,... | collective-permute-start | bytes 884744 | tf_op jit(solution)/shard_map/ppermute | solution.py:13
  112.2 3.4 %copy-start.14 = (bf16[1,1,3,384,384]{4,3,2,1,0:T(8,128)(2,1)S(1)}, bf16[1,1,3,384,384]{4,3,2,1,0:T(8,128)(2,1)}, u32[]{:S(2)}) copy-start(bf16[1,1,3,384,384]{4,3,2,1,0:T(8,128)(2,1)} %get-tuple-element.108) | copy-start | bytes 2654212
  117.8 3.7 %copy-start.2 = (bf16[2,24,32,384]{3,2,1,0:T(8,128)(2,1)S(1)}, bf16[2,24,32,384]{3,2,1,0:T(8,128)(2,1)}, u32[]{:S(2)}) copy-start(bf16[2,24,32,384]{3,2,1,0:T(8,128)(2,1)} %get-tuple-element.110) | copy-start | bytes 3538948
  117.8 3.7 %copy-start.3 = (bf16[2,24,32,384]{3,2,1,0:T(8,128)(2,1)S(1)}, bf16[2,24,32,384]{3,2,1,0:T(8,128)(2,1)}, u32[]{:S(2)}) copy-start(bf16[2,24,32,384]{3,2,1,0:T(8,128)(2,1)} %get-tuple-element.111) | copy-start | bytes 3538948
  117.8 3.7 %copy-start.4 = (bf16[2,24,32,384]{3,2,1,0:T(8,128)(2,1)S(1)}, bf16[2,24,32,384]{3,2,1,0:T(8,128)(2,1)}, u32[]{:S(2)}) copy-start(bf16[2,24,32,384]{3,2,1,0:T(8,128)(2,1)} %get-tuple-element.112) | copy-start | bytes 3538948
  124.6 4.0 %copy-start.11 = (bf16[1,1,3,384,384]{4,3,2,1,0:T(8,128)(2,1)S(1)}, bf16[1,1,3,384,384]{4,3,2,1,0:T(8,128)(2,1)}, u32[]{:S(2)}) copy-start(bf16[1,1,3,384,384]{4,3,2,1,0:T(8,128)(2,1)} %get-tuple-element.105) | copy-start | bytes 2654212
  143.9 20.5 %copy-start.15 = (f32[24]{0:T(128)S(1)}, f32[24]{0:T(128)}, u32[]{:S(2)}) copy-start(f32[24]{0:T(128)} %get-tuple-element.182) | copy-start | bytes 292
  144.4 10.5 %collective-permute-start.8 = (bf16[2,4,4,384]{3,2,1,0:T(4,128)(2,1)S(1)}, bf16[2,4,4,384]{3,2,1,0:T(4,128)(2,1)S(1)}, u32[]{:S(2)}, u32[]{:S(2)}) collective-permute-start(bf16[2,4,4,384]{3,2,1,0:T(4,128)(2,1)S(1)} %get-tuple-element.137), channel_id=1, source_target_pairs={{0,6},{1,7},{8,14},{9,15},{16,22},{17,23},{24,30},{25,31}} | collective-permute-start | bytes 73736 | tf_op jit(solution)/shard_map/ppermute | solution.py:13
  145.7 10.5 %collective-permute-start.15 = (bf16[2,4,4,384]{3,2,1,0:T(4,128)(2,1)S(1)}, bf16[2,4,4,384]{3,2,1,0:T(4,128)(2,1)S(1)}, u32[]{:S(2)}, u32[]{:S(2)}) collective-permute-start(bf16[2,4,4,384]{3,2,1,0:T(4,128)(2,1)S(1)} %get-tuple-element.138), channel_id=1, source_target_pairs={{6,0},{7,1},{14,8},{15,9},{22,16},{23,17},{30,24},{31,25}} | collective-permute-start | bytes 73736 | tf_op jit(solution)/shard_map/ppermute | solution.py:13
  147.0 16.1 %collective-permute-start.13 = (bf16[2,4,4,384]{3,2,1,0:T(4,128)(2,1)S(1)}, bf16[2,4,4,384]{3,2,1,0:T(4,128)(2,1)S(1)}, u32[]{:S(2)}, u32[]{:S(2)}) collective-permute-start(bf16[2,4,4,384]{3,2,1,0:T(4,128)(2,1)S(1)} %get-tuple-element.139), channel_id=1, source_target_pairs={{2,0},{4,2},{6,4},{3,1},{5,3},{7,5},{10,8},{12,10},{14,12},{11,9},... | collective-permute-start | bytes 73736 | tf_op jit(solution)/shard_map/ppermute | solution.py:13
  148.4 16.1 %collective-permute-start.10 = (bf16[2,4,4,384]{3,2,1,0:T(4,128)(2,1)S(1)}, bf16[2,4,4,384]{3,2,1,0:T(4,128)(2,1)S(1)}, u32[]{:S(2)}, u32[]{:S(2)}) collective-permute-start(bf16[2,4,4,384]{3,2,1,0:T(4,128)(2,1)S(1)} %get-tuple-element.140), channel_id=1, source_target_pairs={{0,2},{2,4},{4,6},{1,3},{3,5},{5,7},{8,10},{10,12},{12,14},{9,11},... | collective-permute-start | bytes 73736 | tf_op jit(solution)/shard_map/ppermute | solution.py:13
  152.9 11.6 %collective-permute-start.11 = (bf16[2,16,4,384]{3,2,1,0:T(4,128)(2,1)S(1)}, bf16[2,16,4,384]{3,2,1,0:T(4,128)(2,1)S(1)}, u32[]{:S(2)}, u32[]{:S(2)}) collective-permute-start(bf16[2,16,4,384]{3,2,1,0:T(4,128)(2,1)S(1)} %get-tuple-element.143), channel_id=1, source_target_pairs={{0,2},{2,4},{4,6},{1,3},{3,5},{5,7},{8,10},{10,12},{12,14},{9,11},... | collective-permute-start | bytes 294920 | tf_op jit(solution)/shard_map/ppermute | solution.py:13
  154.9 9.6 %collective-permute-start.12 = (bf16[2,16,4,384]{3,2,1,0:T(4,128)(2,1)S(1)}, bf16[2,16,4,384]{3,2,1,0:T(4,128)(2,1)S(1)}, u32[]{:S(2)}, u32[]{:S(2)}) collective-permute-start(bf16[2,16,4,384]{3,2,1,0:T(4,128)(2,1)S(1)} %get-tuple-element.144), channel_id=1, source_target_pairs={{2,0},{4,2},{6,4},{3,1},{5,3},{7,5},{10,8},{12,10},{14,12},{11,9},... | collective-permute-start | bytes 294920 | tf_op jit(solution)/shard_map/ppermute | solution.py:13
  156.2 9.6 %collective-permute-start.9 = (bf16[2,4,24,384]{3,2,1,0:T(8,128)(2,1)S(1)}, bf16[2,4,24,384]{3,2,1,0:T(8,128)(2,1)S(1)}, u32[]{:S(2)}, u32[]{:S(2)}) collective-permute-start(bf16[2,4,24,384]{3,2,1,0:T(8,128)(2,1)S(1)} %get-tuple-element.141), channel_id=1, source_target_pairs={{0,4},{2,6},{1,5},{3,7},{8,12},{10,14},{9,13},{11,15},{16,20},{18,... | collective-permute-start | bytes 442376 | tf_op jit(solution)/shard_map/ppermute | solution.py:13
  163.1 10.0 %collective-permute-start.14 = (bf16[2,4,24,384]{3,2,1,0:T(8,128)(2,1)S(1)}, bf16[2,4,24,384]{3,2,1,0:T(8,128)(2,1)S(1)}, u32[]{:S(2)}, u32[]{:S(2)}) collective-permute-start(bf16[2,4,24,384]{3,2,1,0:T(8,128)(2,1)S(1)} %get-tuple-element.142), channel_id=1, source_target_pairs={{4,0},{6,2},{5,1},{7,3},{12,8},{14,10},{13,9},{15,11},{20,16},{22,... | collective-permute-start | bytes 442376 | tf_op jit(solution)/shard_map/ppermute | solution.py:13
  (10 other events, 18.4 us)
Sparse Core Ops, SparseCore 0:
  9.2 40.0 all-gather.1
where the time goes:
time: 183 us; the launch traced here: 182 us
  starting transfers between devices  41.4 us (23%)
  waiting for transfers between devices  38.2 us (21%)
  local copies, waits for them, and re-layouts  31.3 us (17%)
  other arithmetic  26.4 us (14%)
  matrix products  22.5 us (12%)
  between operations  22.2 us (12%)
    ppermute x16, starting transfers between devices, passed_along(): return lax.ppermute(shard, axis, pairs)  41.4 us
    dot_general x9, matrix products, convolve(): jnp.dot(flattened, kernel[tap_time, tap_row].reshape(3 * channels, -1), p...  22.5 us
    all_gather x1, waiting for transfers between devices, local(): pieces = lax.all_gather(own_block[None], 'group', axis=0, tiled=True)  20.4 us
    ppermute x16, waiting for transfers between devices, passed_along(): return lax.ppermute(shard, axis, pairs)  17.1 us
    slice x2, local copies, waits for them, and re-layouts, convolve(): window[:, :, tap_col:tap_col + col_count]  10.8 us
    scatter x8, local copies, waits for them, and re-layouts, gather_rims(): result.at[:, row_dest:row_dest + row_len, col_dest:col_dest + col_len]  8.67 us
    another operation x6, other arithmetic  8.1 us
    concatenate x5, other arithmetic, convolve(): jnp.concatenate([window[:, :, tap_col:tap_col + col_count] for tap_col in...  8 us
  transfers between devices with their start and end apart: 17, of which 4 were waited for; matrix products, arithmetic and copies ran while one was open for 16% of the time, Pallas kernels for 0%

commit v1 on v0

--- a/solution.py
+++ b/solution.py
@@ -121,7 +121,14 @@
     reaches = margins[0]
     wanted = group_slot[lax.axis_index("group")] - 1
     chosen = jnp.zeros((2, core_h, core_w, channels), jnp.bfloat16)
-    pieces = lax.all_gather(own_block[None], "group", axis=0, tiled=True)
+    ways, here = (lax.axis_size("group"), lax.axis_index("group"))
+    pieces, reach = (own_block[None], 1)
+    while reach < ways:
+        theirs = lax.ppermute(pieces, "group", [(d, d ^ reach) for d in range(ways)])
+        mine_first = jnp.concatenate([pieces, theirs], axis=0)
+        theirs_first = jnp.concatenate([theirs, pieces], axis=0)
+        pieces = jnp.where(here & reach == 0, mine_first, theirs_first)
+        reach = 2 * reach
     first_dev = jnp.int32(0)
     for offset in range(pieces.shape[0]):
         matches = group_slot[first_dev + offset] == wanted

time: 183 us -> 171 us (0.934)
  between operations: 22.2 us -> 8.72 us
  starting transfers between devices: 41.4 us -> 45 us
  waiting for transfers between devices: 38.2 us -> 35.7 us
    all_gather x1 -> x0, waiting for transfers between devices: 20.4 us -> none  [local(): pieces = lax.all_gather(own_block[None], 'group', axis=0, tiled=True)]
    ppermute x0 -> x2, waiting for transfers between devices: none -> 18.9 us  [local(): lax.ppermute(pieces, 'group', [(d, d ^ reach) for d in range(ways)])]
    ppermute x0 -> x2, starting transfers between devices: none -> 4.8 us  [local(): lax.ppermute(pieces, 'group', [(d, d ^ reach) for d in range(ways)])]
    select_n x0 -> x2, other arithmetic: none -> 1.9 us  [local(): pieces = jnp.where(here & reach == 0, mine_first, theirs_first)]
  transfers between devices with their start and end apart: 17 -> 18, of which waited for: 4 -> 5; matrix products, arithmetic and copies ran while one was open for 16% -> 16% of each run, Pallas kernels for 0% -> 0%
where the time goes in v1:
time: 171 us; the launch traced here: 170 us
  starting transfers between devices  45 us (26%)
  waiting for transfers between devices  35.7 us (21%)
  local copies, waits for them, and re-layouts  32.4 us (19%)
  other arithmetic  25.4 us (15%)
  matrix products  22.5 us (13%)
  between operations  8.72 us (5%)
    ppermute x16, starting transfers between devices, passed_along(): return lax.ppermute(shard, axis, pairs)  40.2 us
    dot_general x9, matrix products, convolve(): jnp.dot(flattened, kernel[tap_time, tap_row].reshape(3 * channels, -1), p...  22.5 us
    ppermute x2, waiting for transfers between devices, local(): lax.ppermute(pieces, 'group', [(d, d ^ reach) for d in range(ways)])  18.9 us
    ppermute x16, waiting for transfers between devices, passed_along(): return lax.ppermute(shard, axis, pairs)  16.9 us
    slice x2, local copies, waits for them, and re-layouts, convolve(): window[:, :, tap_col:tap_col + col_count]  10.8 us
    scatter x8, local copies, waits for them, and re-layouts, gather_rims(): result.at[:, row_dest:row_dest + row_len, col_dest:col_dest + col_len]  8.9 us
    concatenate x5, other arithmetic, convolve(): jnp.concatenate([window[:, :, tap_col:tap_col + col_count] for tap_col in...  7.99 us
    another operation x6, other arithmetic  6.82 us
  transfers between devices with their start and end apart: 18, of which 5 were waited for; matrix products, arithmetic and copies ran while one was open for 16% of the time, Pallas kernels for 0%

profile of v1, /device:TPU:0, one launch (start us, length us, event | category | flops | bytes accessed | tf_op | source)
XLA Modules:
  0.0 169.8 jit_solution(3794315833412526676)
XLA Ops:
  0.0 3.0 %collective-permute-start = (bf16[1,2,16,24,384]{4,3,2,1,0:T(8,128)(2,1)}, bf16[1,2,16,24,384]{4,3,2,1,0:T(8,128)(2,1)S(1)}, u32[]{:S(2)}, u32[]{:S(2)}) collective-permute-start(bf16[1,2,16,24,384]{4,3,2,1,0:T(8,128)(2,1)} %param.22), channel_id=1, source_target_pairs={{0,8},{8,0},{16,24},{24,16},{1,9},{9,1},{17,25},{25,17},{2,10},{10... | collective-permute-start | bytes 1769480 | tf_op jit(solution)/shard_map/ppermute | solution.py:127
  14.2 2.3 %collective-permute-done = bf16[1,2,16,24,384]{4,3,2,1,0:T(8,128)(2,1)S(1)} collective-permute-done((bf16[1,2,16,24,384]{4,3,2,1,0:T(8,128)(2,1)}, bf16[1,2,16,24,384]{4,3,2,1,0:T(8,128)(2,1)S(1)}, u32[]{:S(2)}, u32[]{:S(2)}) %collective-permute-start) | collective-permute-done | bytes 589856 | tf_op jit(solution)/shard_map/ppermute | solution.py:127
  23.0 5.6 %fusion.21 = (bf16[1,1,3,384,384]{4,3,2,1,0:T(8,128)(2,1)}, bf16[1,1,3,384,384]{4,3,2,1,0:T(8,128)(2,1)}, bf16[1,1,3,384,384]{4,3,2,1,0:T(8,128)(2,1)}, bf16[1,1...) fusion(bf16[3,3,3,384,384]{4,3,2,1,0:T(8,128)(2,1)} %param.26), kind=kLoop, calls=%fused_computation.94 | loop fusion | bytes 15925248 | tf_op jit(solution)/shard_map/slice | solution.py:35
  28.6 16.5 %collective-permute-done.1 = bf16[2,2,16,24,384]{4,3,2,1,0:T(8,128)(2,1)S(1)} collective-permute-done((bf16[2,2,16,24,384]{4,3,2,1,0:T(8,128)(2,1)S(1)}, bf16[2,2,16,24,384]{4,3,2,1,0:T(8,128)(2,1)S(1)}, u32[]{:S(2)}, u32[]{:S(2)}) %collective-permute-start.1) | collective-permute-done | bytes 1179680 | tf_op jit(solution)/shard_map/ppermute | solution.py:127
  46.9 4.5 %collective-permute-start.3 = (bf16[4,4,24,384]{3,2,1,0:T(8,128)(2,1)S(1)}, bf16[4,4,24,384]{3,2,1,0:T(8,128)(2,1)S(1)}, u32[]{:S(2)}, u32[]{:S(2)}) collective-permute-start(bf16[4,4,24,384]{3,2,1,0:T(8,128)(2,1)S(1)} %get-tuple-element.150), channel_id=1, source_target_pairs={{0,4},{2,6},{1,5},{3,7},{8,12},{10,14},{9,13},{11,15},{16,20},{18,... | collective-permute-start | bytes 884744 | tf_op jit(solution)/shard_map/ppermute | solution.py:13
  52.1 2.3 %collective-permute-start.2 = (bf16[4,4,4,384]{3,2,1,0:T(4,128)(2,1)S(1)}, bf16[4,4,4,384]{3,2,1,0:T(4,128)(2,1)S(1)}, u32[]{:S(2)}, u32[]{:S(2)}) collective-permute-start(bf16[4,4,4,384]{3,2,1,0:T(4,128)(2,1)S(1)} %get-tuple-element.146), channel_id=1, source_target_pairs={{0,6},{1,7},{8,14},{9,15},{16,22},{17,23},{24,30},{25,31}} | collective-permute-start | bytes 147464 | tf_op jit(solution)/shard_map/ppermute | solution.py:13
  55.9 2.5 %collective-permute-start.4 = (bf16[4,4,4,384]{3,2,1,0:T(4,128)(2,1)}, bf16[4,4,4,384]{3,2,1,0:T(4,128)(2,1)}, u32[]{:S(2)}, u32[]{:S(2)}) collective-permute-start(bf16[4,4,4,384]{3,2,1,0:T(4,128)(2,1)} %get-tuple-element.147), channel_id=1, source_target_pairs={{0,2},{2,4},{4,6},{1,3},{3,5},{5,7},{8,10},{10,12},{12,14},{9,11},... | collective-permute-start | bytes 147464 | tf_op jit(solution)/shard_map/ppermute | solution.py:13
  61.9 5.9 %collective-permute-start.5 = (bf16[4,16,4,384]{3,2,1,0:T(4,128)(2,1)S(1)}, bf16[4,16,4,384]{3,2,1,0:T(4,128)(2,1)}, u32[]{:S(2)}, u32[]{:S(2)}) collective-permute-start(bf16[4,16,4,384]{3,2,1,0:T(4,128)(2,1)S(1)} %get-tuple-element.152), channel_id=1, source_target_pairs={{0,2},{2,4},{4,6},{1,3},{3,5},{5,7},{8,10},{10,12},{12,14},{9,11},... | collective-permute-start | bytes 589832 | tf_op jit(solution)/shard_map/ppermute | solution.py:13
  69.8 2.5 %scatter.29 = bf16[4,24,32,384]{3,2,1,0:T(8,128)(2,1)S(1)} dynamic-update-slice(bf16[4,24,32,384]{3,2,1,0:T(8,128)(2,1)S(1)} %constant_dynamic-update-slice_fusion.4, bf16[4,4,24,384]{3,2,1,0:T(8,128)(2,1)S(1)} %dynamic-slice_select_fusion, s32[]{:T(128)} %constant.277.clone.1, s32[]{:T(128)} %bitcast.10, s32[]{:T(128)} %bitcast.11, s32[]{:T(128)} %constant.277.clone.1) | dynamic-update-slice | bytes 589828 | tf_op jit(solution)/shard_map/scatter | solution.py:111
  73.9 3.3 %dynamic-slice_select_fusion.1 = bf16[4,4,4,384]{3,2,1,0:T(4,128)(2,1)} fusion(bf16[4,4,4,384]{3,2,1,0:T(4,128)(2,1)} %collective-permute-done.4, bf16[4,24,32,384]{3,2,1,0:T(8,128)(2,1)S(1)} %scatter.29, s32[]{:T(128)} %bitcast.12, s32[]{:T(128)} %bitcast.13, pred[]{:T(512)} %and_reduce_fusion), kind=kLoop, calls=%fused_computation.68 | loop fusion | flops 24576 | bytes 147465 | tf_op jit(solution)/shard_map/select.10
  77.2 2.2 %scatter.30 = bf16[4,24,32,384]{3,2,1,0:T(8,128)(2,1)S(1)} dynamic-update-slice(bf16[4,24,32,384]{3,2,1,0:T(8,128)(2,1)S(1)} %scatter.29, bf16[4,4,4,384]{3,2,1,0:T(4,128)(2,1)} %dynamic-slice_select_fusion.1, s32[]{:T(128)} %constant.277.clone.1, s32[]{:T(128)} %bitcast.12, s32[]{:T(128)} %bitcast.13, s32[]{:T(128)} %constant.277.clone.1) | dynamic-update-slice | bytes 98308 | tf_op jit(solution)/shard_map/scatter | solution.py:111
  81.5 8.3 %collective-permute-done.8 = bf16[4,4,24,384]{3,2,1,0:T(8,128)(2,1)S(1)} collective-permute-done((bf16[4,4,24,384]{3,2,1,0:T(8,128)(2,1)S(1)}, bf16[4,4,24,384]{3,2,1,0:T(8,128)(2,1)S(1)}, u32[]{:S(2)}, u32[]{:S(2)}) %collective-permute-start.8) | collective-permute-done | bytes 294944 | tf_op jit(solution)/shard_map/ppermute | solution.py:13
  92.4 2.2 %fusion.7 = bf16[4,24,32,384]{3,2,1,0:T(8,128)(2,1)S(1)} fusion(bf16[4,24,32,384]{3,2,1,0:T(8,128)(2,1)S(1)} %constant_dynamic-update-slice_fusion, f32[384]{0:T(512)} %param.25, f32[4,24,32]{2,1,0:T(8,128)S(1)} %add_rsqrt_fusion), kind=kLoop, calls=%fused_computation.9 | loop fusion | flops 9437184 | bytes 4732416 | tf_op jit(solution)/shard_map/convert_element_type | solution.py:19
  96.1 4.5 %fusion.23 = (bf16[2,24,32,384]{3,2,1,0:T(8,128)(2,1)S(1)}, bf16[2,24,32,384]{3,2,1,0:T(8,128)(2,1)S(1)}, bf16[2,24,32,384]{3,2,1,0:T(8,128)(2,1)}, bf16[2,24,32...) fusion(bf16[4,26,34,384]{3,2,1,0:T(8,128)(2,1)S(1)} %pad_select, ...), kind=kLoop, calls=%fused_computation.96 | loop fusion | bytes 18874368 | tf_op jit(solution)/shard_map/slice | solution.py:30
  100.6 6.3 %fusion.22 = (bf16[2,24,32,384]{3,2,1,0:T(8,128)(2,1)}, bf16[2,24,32,384]{3,2,1,0:T(8,128)(2,1)}, bf16[2,24,32,384]{3,2,1,0:T(8,128)(2,1)}, bf16[2,24,32,384]{3,...) fusion(bf16[4,26,34,384]{3,2,1,0:T(8,128)(2,1)S(1)} %pad_select, ...), kind=kLoop, calls=%fused_computation.95 | loop fusion | bytes 44826624 | tf_op jit(solution)/shard_map/slice | solution.py:30
  106.9 3.4 %pad_maximum_fusion = (bf16[2,24,32,1152]{3,2,1,0:T(8,128)(2,1)S(1)}, bf16[2,24,32,1152]{3,2,1,0:T(8,128)(2,1)S(1)}) fusion(bf16[2,24,32,384]{3,2,1,0:T(8,128)(2,1)} %get-tuple-element.134, bf16[2,24,32,384]{3,2,1,0:T(8,128)(2,1)} %get-tuple-element.135, bf16[2,24,32,384]{3,2,1,0:T(8,128)(2,1)} %get-tuple-element.136, ...), kind=kLoop, calls=%fused_computation.10 | loop fusion | flops 21233664 | bytes 14155776 | tf_op jit(solution)/shard_map/concatenate | solution.py:29
  112.5 3.6 %convolution_add_fusion.7 = f32[1536,384]{1,0:T(8,128)} fusion(f32[1536,384]{1,0:T(8,128)S(1)} %fusion.31, bf16[1536,1152]{1,0:T(8,128)(2,1)S(1)} %bitcast.65, bf16[1152,384]{1,0:T(8,128)(2,1)S(1)} %bitcast.79), kind=kOutput, calls=%fused_computation.27 | convolution fusion | flops 1359544320 | bytes 9142272 | tf_op jit(solution)/shard_map/dot_general | solution.py:33
  119.2 3.9 %convolution_add_fusion.6 = f32[1536,384]{1,0:T(8,128)S(1)} fusion(f32[1536,384]{1,0:T(8,128)} %convolution_add_fusion.7, bf16[1536,1152]{1,0:T(8,128)(2,1)S(1)} %bitcast.66, bf16[1152,384]{1,0:T(8,128)(2,1)S(1)} %bitcast.78), kind=kOutput, calls=%fused_computation.26 | convolution fusion | flops 1359544320 | bytes 9142272 | tf_op jit(solution)/shard_map/dot_general | solution.py:33
  123.2 2.2 %convolution_add_fusion.5 = f32[1536,384]{1,0:T(8,128)S(1)} fusion(f32[1536,384]{1,0:T(8,128)S(1)} %convolution_add_fusion.6, bf16[1536,1152]{1,0:T(8,128)(2,1)S(1)} %bitcast.62, bf16[1152,384]{1,0:T(8,128)(2,1)S(1)} %bitcast.77), kind=kOutput, calls=%fused_computation.25 | convolution fusion | flops 1359544320 | bytes 9142272 | tf_op jit(solution)/shard_map/dot_general | solution.py:33
  126.5 2.2 %convolution_add_fusion.4 = f32[1536,384]{1,0:T(8,128)S(1)} fusion(f32[1536,384]{1,0:T(8,128)S(1)} %convolution_add_fusion.5, bf16[1536,1152]{1,0:T(8,128)(2,1)S(1)} %bitcast.67, bf16[1152,384]{1,0:T(8,128)(2,1)S(1)} %bitcast.76), kind=kOutput, calls=%fused_computation.24 | convolution fusion | flops 1359544320 | bytes 9142272 | tf_op jit(solution)/shard_map/dot_general | solution.py:33
  132.0 2.2 %convolution_add_fusion.2 = f32[1536,384]{1,0:T(8,128)S(1)} fusion(f32[1536,384]{1,0:T(8,128)S(1)} %convolution_add_fusion.3, bf16[1536,1152]{1,0:T(8,128)(2,1)S(1)} %bitcast.68, bf16[1152,384]{1,0:T(8,128)(2,1)S(1)} %bitcast.74), kind=kOutput, calls=%fused_computation.22 | convolution fusion | flops 1359544320 | bytes 9142272 | tf_op jit(solution)/shard_map/dot_general | solution.py:33
  143.0 4.5 %collective-permute-start.12 = (bf16[2,4,4,384]{3,2,1,0:T(4,128)(2,1)S(1)}, bf16[2,4,4,384]{3,2,1,0:T(4,128)(2,1)S(1)}, u32[]{:S(2)}, u32[]{:S(2)}) collective-permute-start(bf16[2,4,4,384]{3,2,1,0:T(4,128)(2,1)S(1)} %get-tuple-element.140), channel_id=1, source_target_pairs={{0,2},{2,4},{4,6},{1,3},{3,5},{5,7},{8,10},{10,12},{12,14},{9,11},... | collective-permute-start | bytes 73736 | tf_op jit(solution)/shard_map/ppermute | solution.py:13
  150.8 6.9 %collective-permute-start.11 = (bf16[2,4,24,384]{3,2,1,0:T(8,128)(2,1)S(1)}, bf16[2,4,24,384]{3,2,1,0:T(8,128)(2,1)S(1)}, u32[]{:S(2)}, u32[]{:S(2)}) collective-permute-start(bf16[2,4,24,384]{3,2,1,0:T(8,128)(2,1)S(1)} %get-tuple-element.141), channel_id=1, source_target_pairs={{0,4},{2,6},{1,5},{3,7},{8,12},{10,14},{9,13},{11,15},{16,20},{18,... | collective-permute-start | bytes 442376 | tf_op jit(solution)/shard_map/ppermute | solution.py:13
  160.4 7.4 %collective-permute-done.16 = bf16[2,4,24,384]{3,2,1,0:T(8,128)(2,1)S(1)} collective-permute-done((bf16[2,4,24,384]{3,2,1,0:T(8,128)(2,1)S(1)}, bf16[2,4,24,384]{3,2,1,0:T(8,128)(2,1)S(1)}, u32[]{:S(2)}, u32[]{:S(2)}) %collective-permute-start.16) | collective-permute-done | bytes 147488 | tf_op jit(solution)/shard_map/ppermute | solution.py:13
  (109 shorter events, 53.0 us)
Async XLA Ops:
  0.0 21.6 %copy-start.18 = (s32[4]{0:T(128)S(1)}, s32[4]{0:T(128)}, u32[]{:S(2)}) copy-start(s32[4]{0:T(128)} %constant.284.clone.1) | copy-start | bytes 52
  0.0 22.3 %copy-start.17 = (s32[4]{0:T(128)S(1)}, s32[4]{0:T(128)}, u32[]{:S(2)}) copy-start(s32[4]{0:T(128)} %constant.287.clone.1) | copy-start | bytes 52
  0.0 16.5 %collective-permute-start = (bf16[1,2,16,24,384]{4,3,2,1,0:T(8,128)(2,1)}, bf16[1,2,16,24,384]{4,3,2,1,0:T(8,128)(2,1)S(1)}, u32[]{:S(2)}, u32[]{:S(2)}) collective-permute-start(bf16[1,2,16,24,384]{4,3,2,1,0:T(8,128)(2,1)} %param.22), channel_id=1, source_target_pairs={{0,8},{8,0},{16,24},{24,16},{1,9},{9,1},{17,25},{25,17},{2,10},{10... | collective-permute-start | bytes 1769480 | tf_op jit(solution)/shard_map/ppermute | solution.py:127
  18.0 27.2 %collective-permute-start.1 = (bf16[2,2,16,24,384]{4,3,2,1,0:T(8,128)(2,1)S(1)}, bf16[2,2,16,24,384]{4,3,2,1,0:T(8,128)(2,1)S(1)}, u32[]{:S(2)}, u32[]{:S(2)}) collective-permute-start(bf16[2,2,16,24,384]{4,3,2,1,0:T(8,128)(2,1)S(1)} %maximum_select_fusion.1), channel_id=1, source_target_pairs={{0,16},{8,24},{16,0},{24,8},{1,17},{9,25},{17,1},{25,9},{2,18},{10... | collective-permute-start | bytes 3538952 | tf_op jit(solution)/shard_map/ppermute | solution.py:127
  46.9 15.0 %collective-permute-start.3 = (bf16[4,4,24,384]{3,2,1,0:T(8,128)(2,1)S(1)}, bf16[4,4,24,384]{3,2,1,0:T(8,128)(2,1)S(1)}, u32[]{:S(2)}, u32[]{:S(2)}) collective-permute-start(bf16[4,4,24,384]{3,2,1,0:T(8,128)(2,1)S(1)} %get-tuple-element.150), channel_id=1, source_target_pairs={{0,4},{2,6},{1,5},{3,7},{8,12},{10,14},{9,13},{11,15},{16,20},{18,... | collective-permute-start | bytes 884744 | tf_op jit(solution)/shard_map/ppermute | solution.py:13
  52.1 8.4 %collective-permute-start.2 = (bf16[4,4,4,384]{3,2,1,0:T(4,128)(2,1)S(1)}, bf16[4,4,4,384]{3,2,1,0:T(4,128)(2,1)S(1)}, u32[]{:S(2)}, u32[]{:S(2)}) collective-permute-start(bf16[4,4,4,384]{3,2,1,0:T(4,128)(2,1)S(1)} %get-tuple-element.146), channel_id=1, source_target_pairs={{0,6},{1,7},{8,14},{9,15},{16,22},{17,23},{24,30},{25,31}} | collective-permute-start | bytes 147464 | tf_op jit(solution)/shard_map/ppermute | solution.py:13
  54.6 36.3 %collective-permute-start.9 = (bf16[4,4,4,384]{3,2,1,0:T(4,128)(2,1)}, bf16[4,4,4,384]{3,2,1,0:T(4,128)(2,1)}, u32[]{:S(2)}, u32[]{:S(2)}) collective-permute-start(bf16[4,4,4,384]{3,2,1,0:T(4,128)(2,1)} %get-tuple-element.145), channel_id=1, source_target_pairs={{6,0},{7,1},{14,8},{15,9},{22,16},{23,17},{30,24},{31,25}} | collective-permute-start | bytes 147464 | tf_op jit(solution)/shard_map/ppermute | solution.py:13
  55.9 16.4 %collective-permute-start.4 = (bf16[4,4,4,384]{3,2,1,0:T(4,128)(2,1)}, bf16[4,4,4,384]{3,2,1,0:T(4,128)(2,1)}, u32[]{:S(2)}, u32[]{:S(2)}) collective-permute-start(bf16[4,4,4,384]{3,2,1,0:T(4,128)(2,1)} %get-tuple-element.147), channel_id=1, source_target_pairs={{0,2},{2,4},{4,6},{1,3},{3,5},{5,7},{8,10},{10,12},{12,14},{9,11},... | collective-permute-start | bytes 147464 | tf_op jit(solution)/shard_map/ppermute | solution.py:13
  58.4 22.3 %collective-permute-start.7 = (bf16[4,4,4,384]{3,2,1,0:T(4,128)(2,1)}, bf16[4,4,4,384]{3,2,1,0:T(4,128)(2,1)}, u32[]{:S(2)}, u32[]{:S(2)}) collective-permute-start(bf16[4,4,4,384]{3,2,1,0:T(4,128)(2,1)} %get-tuple-element.148), channel_id=1, source_target_pairs={{2,0},{4,2},{6,4},{3,1},{5,3},{7,5},{10,8},{12,10},{14,12},{11,9},... | collective-permute-start | bytes 147464 | tf_op jit(solution)/shard_map/ppermute | solution.py:13
  60.5 20.0 %collective-permute-start.6 = (bf16[4,16,4,384]{3,2,1,0:T(4,128)(2,1)S(1)}, bf16[4,16,4,384]{3,2,1,0:T(4,128)(2,1)S(1)}, u32[]{:S(2)}, u32[]{:S(2)}) collective-permute-start(bf16[4,16,4,384]{3,2,1,0:T(4,128)(2,1)S(1)} %get-tuple-element.151), channel_id=1, source_target_pairs={{2,0},{4,2},{6,4},{3,1},{5,3},{7,5},{10,8},{12,10},{14,12},{11,9},... | collective-permute-start | bytes 589832 | tf_op jit(solution)/shard_map/ppermute | solution.py:13
  61.9 17.5 %collective-permute-start.5 = (bf16[4,16,4,384]{3,2,1,0:T(4,128)(2,1)S(1)}, bf16[4,16,4,384]{3,2,1,0:T(4,128)(2,1)}, u32[]{:S(2)}, u32[]{:S(2)}) collective-permute-start(bf16[4,16,4,384]{3,2,1,0:T(4,128)(2,1)S(1)} %get-tuple-element.152), channel_id=1, source_target_pairs={{0,2},{2,4},{4,6},{1,3},{3,5},{5,7},{8,10},{10,12},{12,14},{9,11},... | collective-permute-start | bytes 589832 | tf_op jit(solution)/shard_map/ppermute | solution.py:13
  72.4 17.4 %collective-permute-start.8 = (bf16[4,4,24,384]{3,2,1,0:T(8,128)(2,1)S(1)}, bf16[4,4,24,384]{3,2,1,0:T(8,128)(2,1)S(1)}, u32[]{:S(2)}, u32[]{:S(2)}) collective-permute-start(bf16[4,4,24,384]{3,2,1,0:T(8,128)(2,1)S(1)} %get-tuple-element.149), channel_id=1, source_target_pairs={{4,0},{6,2},{5,1},{7,3},{12,8},{14,10},{13,9},{15,11},{20,16},{22,... | collective-permute-start | bytes 884744 | tf_op jit(solution)/shard_map/ppermute | solution.py:13
  112.5 3.7 %copy-start.2 = (bf16[2,24,32,384]{3,2,1,0:T(8,128)(2,1)S(1)}, bf16[2,24,32,384]{3,2,1,0:T(8,128)(2,1)}, u32[]{:S(2)}) copy-start(bf16[2,24,32,384]{3,2,1,0:T(8,128)(2,1)} %get-tuple-element.110) | copy-start | bytes 3538948
  112.5 3.7 %copy-start.3 = (bf16[2,24,32,384]{3,2,1,0:T(8,128)(2,1)S(1)}, bf16[2,24,32,384]{3,2,1,0:T(8,128)(2,1)}, u32[]{:S(2)}) copy-start(bf16[2,24,32,384]{3,2,1,0:T(8,128)(2,1)} %get-tuple-element.111) | copy-start | bytes 3538948
  119.2 3.9 %copy-start.11 = (bf16[1,1,3,384,384]{4,3,2,1,0:T(8,128)(2,1)S(1)}, bf16[1,1,3,384,384]{4,3,2,1,0:T(8,128)(2,1)}, u32[]{:S(2)}) copy-start(bf16[1,1,3,384,384]{4,3,2,1,0:T(8,128)(2,1)} %get-tuple-element.105) | copy-start | bytes 2654212
  138.6 20.5 %copy-start.15 = (f32[24]{0:T(128)S(1)}, f32[24]{0:T(128)}, u32[]{:S(2)}) copy-start(f32[24]{0:T(128)} %get-tuple-element.182) | copy-start | bytes 292
  139.0 10.5 %collective-permute-start.10 = (bf16[2,4,4,384]{3,2,1,0:T(4,128)(2,1)S(1)}, bf16[2,4,4,384]{3,2,1,0:T(4,128)(2,1)S(1)}, u32[]{:S(2)}, u32[]{:S(2)}) collective-permute-start(bf16[2,4,4,384]{3,2,1,0:T(4,128)(2,1)S(1)} %get-tuple-element.137), channel_id=1, source_target_pairs={{0,6},{1,7},{8,14},{9,15},{16,22},{17,23},{24,30},{25,31}} | collective-permute-start | bytes 73736 | tf_op jit(solution)/shard_map/ppermute | solution.py:13
  140.3 10.5 %collective-permute-start.17 = (bf16[2,4,4,384]{3,2,1,0:T(4,128)(2,1)S(1)}, bf16[2,4,4,384]{3,2,1,0:T(4,128)(2,1)S(1)}, u32[]{:S(2)}, u32[]{:S(2)}) collective-permute-start(bf16[2,4,4,384]{3,2,1,0:T(4,128)(2,1)S(1)} %get-tuple-element.138), channel_id=1, source_target_pairs={{6,0},{7,1},{14,8},{15,9},{22,16},{23,17},{30,24},{31,25}} | collective-permute-start | bytes 73736 | tf_op jit(solution)/shard_map/ppermute | solution.py:13
  141.6 16.1 %collective-permute-start.15 = (bf16[2,4,4,384]{3,2,1,0:T(4,128)(2,1)S(1)}, bf16[2,4,4,384]{3,2,1,0:T(4,128)(2,1)S(1)}, u32[]{:S(2)}, u32[]{:S(2)}) collective-permute-start(bf16[2,4,4,384]{3,2,1,0:T(4,128)(2,1)S(1)} %get-tuple-element.139), channel_id=1, source_target_pairs={{2,0},{4,2},{6,4},{3,1},{5,3},{7,5},{10,8},{12,10},{14,12},{11,9},... | collective-permute-start | bytes 73736 | tf_op jit(solution)/shard_map/ppermute | solution.py:13
  143.0 16.1 %collective-permute-start.12 = (bf16[2,4,4,384]{3,2,1,0:T(4,128)(2,1)S(1)}, bf16[2,4,4,384]{3,2,1,0:T(4,128)(2,1)S(1)}, u32[]{:S(2)}, u32[]{:S(2)}) collective-permute-start(bf16[2,4,4,384]{3,2,1,0:T(4,128)(2,1)S(1)} %get-tuple-element.140), channel_id=1, source_target_pairs={{0,2},{2,4},{4,6},{1,3},{3,5},{5,7},{8,10},{10,12},{12,14},{9,11},... | collective-permute-start | bytes 73736 | tf_op jit(solution)/shard_map/ppermute | solution.py:13
  147.6 11.6 %collective-permute-start.13 = (bf16[2,16,4,384]{3,2,1,0:T(4,128)(2,1)S(1)}, bf16[2,16,4,384]{3,2,1,0:T(4,128)(2,1)S(1)}, u32[]{:S(2)}, u32[]{:S(2)}) collective-permute-start(bf16[2,16,4,384]{3,2,1,0:T(4,128)(2,1)S(1)} %get-tuple-element.143), channel_id=1, source_target_pairs={{0,2},{2,4},{4,6},{1,3},{3,5},{5,7},{8,10},{10,12},{12,14},{9,11},... | collective-permute-start | bytes 294920 | tf_op jit(solution)/shard_map/ppermute | solution.py:13
  149.5 9.6 %collective-permute-start.14 = (bf16[2,16,4,384]{3,2,1,0:T(4,128)(2,1)S(1)}, bf16[2,16,4,384]{3,2,1,0:T(4,128)(2,1)S(1)}, u32[]{:S(2)}, u32[]{:S(2)}) collective-permute-start(bf16[2,16,4,384]{3,2,1,0:T(4,128)(2,1)S(1)} %get-tuple-element.144), channel_id=1, source_target_pairs={{2,0},{4,2},{6,4},{3,1},{5,3},{7,5},{10,8},{12,10},{14,12},{11,9},... | collective-permute-start | bytes 294920 | tf_op jit(solution)/shard_map/ppermute | solution.py:13
  150.8 9.6 %collective-permute-start.11 = (bf16[2,4,24,384]{3,2,1,0:T(8,128)(2,1)S(1)}, bf16[2,4,24,384]{3,2,1,0:T(8,128)(2,1)S(1)}, u32[]{:S(2)}, u32[]{:S(2)}) collective-permute-start(bf16[2,4,24,384]{3,2,1,0:T(8,128)(2,1)S(1)} %get-tuple-element.141), channel_id=1, source_target_pairs={{0,4},{2,6},{1,5},{3,7},{8,12},{10,14},{9,13},{11,15},{16,20},{18,... | collective-permute-start | bytes 442376 | tf_op jit(solution)/shard_map/ppermute | solution.py:13
  157.7 10.0 %collective-permute-start.16 = (bf16[2,4,24,384]{3,2,1,0:T(8,128)(2,1)S(1)}, bf16[2,4,24,384]{3,2,1,0:T(8,128)(2,1)S(1)}, u32[]{:S(2)}, u32[]{:S(2)}) collective-permute-start(bf16[2,4,24,384]{3,2,1,0:T(8,128)(2,1)S(1)} %get-tuple-element.142), channel_id=1, source_target_pairs={{4,0},{6,2},{5,1},{7,3},{12,8},{14,10},{13,9},{15,11},{20,16},{22,... | collective-permute-start | bytes 442376 | tf_op jit(solution)/shard_map/ppermute | solution.py:13
  (13 other events, 26.6 us)
